TPU v7x, 32 devices: a whole 2x2x4 slice. The times are simulated.
32 devices in a mesh: groups: 2 (over x), ctx: 16 (over z, y, core).
Axes of the slice: x: 2, y: 2, z: 4, core: 2. Of those that a mesh axis runs over, the one named last changes fastest.
Arguments:
- queries: bfloat16 [128, 4096], P(('groups', 'ctx')), parts along dimension 0, may hold values from -110 to 110
- keys: bfloat16 [16, 65536, 128], P(None, ('groups', 'ctx')), parts along dimension 1, may hold values from -8 to 8
- values: bfloat16 [16, 65536, 128], P(None, ('groups', 'ctx')), parts along dimension 1, may hold values from -6 to 6
- residual: bfloat16 [128, 5376], P(('groups', 'ctx')), parts along dimension 0, may hold values from -6 to 6
- post_gain: float32 [5376], replicated, may hold values from 0.5 to 1.5
- out_weight: bfloat16 [4096, 5376], P('ctx'), may hold values from -0.09375 to 0.09375
Outputs:
- updated: float32 [128, 5376], P(('groups', 'ctx')), parts along dimension 0
There are 2 independent parts, one for each index of `groups`. A program takes and returns all parts, laid end to end along the dimension named above; an argument that names none is the same for every part. Nothing has to cross between parts.
All inputs are finite; a program needn't handle non-finite values.
Results may differ from a plain program's by a relative error of at most 0.017.
Values may be sent and summed in bfloat16 or wider, within the bound.
No kernel may reach another device: no remote copies, remote signals or barrier semaphores. Data moves between devices by JAX's collectives and lax.ppermute only.
A program may use at most 320 MiB of HBM per device.

v0:
```python
import functools
import math

import jax
import jax.numpy as jnp
from jax import lax
from jax.experimental import pallas as pl
from jax.experimental.pallas import tpu as pltpu
from jax.sharding import PartitionSpec as P


SCALE = 168.0 ** (-0.5)
EXPONENT_SCALE = SCALE * math.log2(math.e)
EPSILON = 1e-06
AUX = 8
CHUNK = 2048
VMEM_SPEC = pl.BlockSpec(memory_space=pltpu.VMEM)


def params(limit=8 << 20):
    return pltpu.CompilerParams(vmem_limit_bytes=limit)


def split_pieces(x, count):
    pieces = []
    for _ in range(count):
        piece = x.astype(jnp.bfloat16)
        pieces.append(piece)
        x = x - piece.astype(jnp.float32)
    return pieces


def pack_aux(peak, total):
    rows = split_pieces(peak, 3) + split_pieces(total, 2)
    rows = [row.astype(jnp.float32) for row in rows]
    rows.append(jnp.zeros((AUX - len(rows), peak.shape[1]), jnp.float32))
    return jnp.concatenate(rows, axis=0).astype(jnp.bfloat16)


def unpack_aux(aux):
    aux = aux.astype(jnp.float32)
    peak = (aux[0:1] + aux[1:2]) + aux[2:3]
    total = aux[3:4] + aux[4:5]
    return peak, total


def slot_of(offset):
    return lax.bitwise_xor(lax.rem(lax.axis_index("ctx"), 4), offset)


def fetch_kernel(in_ref, out_ref, sem):
    copy = pltpu.make_async_copy(in_ref, out_ref, sem)
    copy.start()
    copy.wait()


def fetch(x):
    return pl.pallas_call(
        fetch_kernel,
        out_shape=jax.ShapeDtypeStruct(x.shape, x.dtype),
        in_specs=[pl.BlockSpec(memory_space=pltpu.HBM)],
        out_specs=VMEM_SPEC,
        scratch_shapes=[pltpu.SemaphoreType.DMA],
        compiler_params=params(2 << 20),
        cost_estimate=pl.CostEstimate(
            flops=0, bytes_accessed=64 * x.size * x.dtype.itemsize, transcendentals=0
        ),
    )(pltpu.with_memory_space_constraint(x, pltpu.HBM))


def spread_kernel(own_width, own_ref, partner_ref, out_ref):
    chips = out_ref.shape[0]
    slot = slot_of(1)
    parity = lax.rem(slot, 2)
    for p in range(chips):
        start = pl.multiple_of((2 * p + parity) * own_width, own_width)
        own = own_ref[:, pl.ds(start, own_width)].astype(jnp.float32)
        partner = partner_ref[:, pl.ds(start, own_width)].astype(jnp.float32)
        first = jnp.where(parity == 1, own, partner)
        second = jnp.where(parity == 1, partner, own)
        block = jnp.concatenate([first, second], axis=0).astype(jnp.bfloat16)
        for q in range(chips):
            place = p // 2 + (chips // 2 if p % 2 == q % 2 else 0)
            out_ref[q, :, place * own_width : (place + 1) * own_width] = block


def spread(queries, partner_queries, chips, own_width, cover):
    return pl.pallas_call(
        functools.partial(spread_kernel, own_width),
        out_shape=jax.ShapeDtypeStruct(
            (chips, 2 * queries.shape[0], chips * own_width), queries.dtype
        ),
        in_specs=[VMEM_SPEC] * 2,
        out_specs=VMEM_SPEC,
        compiler_params=params(2 << 20),
        cost_estimate=pl.CostEstimate(flops=cover, bytes_accessed=0, transcendentals=0),
    )(queries, partner_queries)


def attend_kernel(
    offset, few, own_heads, heads, group, head_dim, chunk, tasks,
    q_ref, k_ref, v_ref, *refs,
):
    out_ref, score_a, score_b = refs[-3:]
    positions = k_ref.shape[1]
    per_device = own_heads // heads
    slot = slot_of(offset)

    def first_head(t):
        device = 4 * (t // per_device) + slot
        return device * own_heads + (t % per_device) * heads

    def load_query(t):
        first = t * heads + (0 if offset >= 2 else tasks * heads)
        columns = [
            q_ref[:, (first + g) * head_dim : (first + g + 1) * head_dim].astype(jnp.float32)
            for g in range(heads)
        ]
        rows = [
            column[start + core * few : start + (core + 1) * few]
            for core in range(2)
            for column in columns
            for start in range(0, q_ref.shape[0], 2 * few)
        ]
        return jnp.concatenate(rows, axis=0).astype(jnp.bfloat16)

    def score(q, kv, start, score_ref):
        part = lax.dot_general(
            q,
            k_ref[kv, start : start + chunk, :],
            (((1,), (1,)), ((), ())),
            preferred_element_type=jnp.float32,
        )
        score_ref[:, start : start + chunk] = part
        tiles = [part[:, i : i + 128] for i in range(0, chunk, 128)]
        return functools.reduce(jnp.maximum, tiles)

    def weigh(kv, peak, start, score_ref):
        exponent = jnp.exp2((score_ref[:, start : start + chunk] - peak) * EXPONENT_SCALE)
        tiles = [exponent[:, i : i + 128] for i in range(0, chunk, 128)]
        weighted = jnp.dot(
            exponent.astype(jnp.bfloat16),
            v_ref[kv, start : start + chunk, :],
            preferred_element_type=jnp.float32,
        )
        return functools.reduce(jnp.add, tiles), weighted

    def section(t, peak, current_ref, following, next_ref):
        kv = first_head(t) // group
        if following is not None:
            q, next_kv = load_query(following), first_head(following) // group
        highest = total = weighted = None
        for start in range(0, positions, chunk):
            if following is not None:
                part = score(q, next_kv, start, next_ref)
                highest = part if highest is None else jnp.maximum(highest, part)
            exponents, product = weigh(kv, peak, start, current_ref)
            total = exponents if total is None else total + exponents
            weighted = product if weighted is None else weighted + product
        total = jnp.sum(total, axis=1, keepdims=True)
        out_ref[t, 0:head_dim, :] = weighted.T.astype(jnp.bfloat16)
        lane = lax.broadcasted_iota(jnp.int32, (peak.shape[0], 128), 1)
        stats = jnp.where(lane == 0, peak, total).T
        out_ref[t, head_dim : head_dim + AUX, :] = pack_aux(stats[0:1], stats[1:2])
        return None if highest is None else jnp.max(highest, axis=1, keepdims=True)

    q = load_query(0)
    highest = None
    for start in range(0, positions, chunk):
        part = score(q, first_head(0) // group, start, score_a)
        highest = part if highest is None else jnp.maximum(highest, part)
    peak = jnp.max(highest, axis=1, keepdims=True)

    for t in range(tasks):
        score_refs = (score_a, score_b) if t % 2 == 0 else (score_b, score_a)
        peak = section(t, peak, score_refs[0], t + 1 if t + 1 < tasks else None, score_refs[1])


def attend(offset, queries, keys, values, few, own_heads, head_count, after):
    kv_heads, positions, head_dim = keys.shape
    units = queries.shape[0]
    group = head_count // kv_heads
    heads = min(group, own_heads)
    tasks = head_count // (4 * heads)
    rows = units * heads
    return pl.pallas_call(
        functools.partial(
            attend_kernel, offset, few, own_heads, heads, group, head_dim, min(CHUNK, positions), tasks
        ),
        out_shape=jax.ShapeDtypeStruct((tasks, head_dim + AUX, rows), jnp.bfloat16),
        in_specs=[VMEM_SPEC] * (3 + len(after)),
        out_specs=VMEM_SPEC,
        scratch_shapes=[pltpu.VMEM((rows, positions), jnp.float32)] * 2,
        compiler_params=params(20 << 20),
        cost_estimate=pl.CostEstimate(
            flops=4 * tasks * rows * positions * head_dim,
            bytes_accessed=4 * tasks * positions * head_dim,
            transcendentals=tasks * rows * positions,
        ),
    )(queries, keys, values, *after)


def join(head_dim, parts):
    stats = [unpack_aux(part[head_dim : head_dim + AUX, :]) for part in parts]
    peak = functools.reduce(jnp.maximum, [s[0] for s in stats])
    scales = [jnp.exp2((s[0] - peak) * EXPONENT_SCALE) for s in stats]
    total = functools.reduce(jnp.add, [s[1] * x for s, x in zip(stats, scales)])
    weighted = [
        part[0:head_dim, :].astype(jnp.float32) * x for part, x in zip(parts, scales)
    ]
    return peak, total, functools.reduce(jnp.add, weighted)


def combine_kernel(head_dim, *refs):
    out_ref = refs[-1]
    for t in range(out_ref.shape[0]):
        peak, total, weighted = join(head_dim, [ref.at[t] for ref in refs[:-1]])
        out_ref[t, 0:head_dim, :] = weighted.astype(jnp.bfloat16)
        out_ref[t, head_dim : head_dim + AUX, :] = pack_aux(peak, total)


def combine(head_dim, *parts):
    return pl.pallas_call(
        functools.partial(combine_kernel, head_dim),
        out_shape=jax.ShapeDtypeStruct(parts[0].shape, jnp.bfloat16),
        in_specs=[VMEM_SPEC] * len(parts),
        out_specs=VMEM_SPEC,
        compiler_params=params(),
    )(*parts)


def pack_kernel(head_dim, *refs):
    out_ref = refs[-1]
    per_device = out_ref.shape[2]
    half = head_dim // 2
    for t in range(refs[0].shape[0]):
        peak, total, weighted = join(head_dim, [ref.at[t] for ref in refs[:-1]])
        aux = pack_aux(peak, total).astype(jnp.float32)
        units = aux.shape[1] // 2
        for core in range(2):
            lanes = slice(core * units, (core + 1) * units)
            top, bottom = weighted[0:half, lanes], weighted[half:head_dim, lanes]
            cut = out_ref.at[t // per_device, core, t % per_device]
            cut[0:half, :] = jnp.concatenate([top, bottom], axis=1).astype(jnp.bfloat16)
            pair = jnp.concatenate([aux[:, lanes], aux[:, lanes]], axis=1)
            cut[half : half + AUX, :] = pair.astype(jnp.bfloat16)


def pack(head_dim, planes, *parts):
    tasks, _, rows = parts[0].shape
    shape = (planes, 2, tasks // planes, head_dim // 2 + AUX, rows)
    return pl.pallas_call(
        functools.partial(pack_kernel, head_dim),
        out_shape=jax.ShapeDtypeStruct(shape, jnp.bfloat16),
        in_specs=[VMEM_SPEC] * len(parts),
        out_specs=VMEM_SPEC,
        compiler_params=params(),
    )(*parts)


def project_kernel(heads, head_dim, tile, part_ref, weight_ref, partner_ref, out_ref, lhs_ref):
    sources, per_device, _, rows = part_ref.shape
    chips, few, width = out_ref.shape
    half = head_dim // 2
    parity = lax.rem(lax.axis_index("ctx"), 2)
    for side in range(2):
        core = lax.rem(parity + side, 2)
        for j in range(per_device):
            parts = [part_ref.at[2 * z + core, j] for z in range(sources // 2)]
            _, total, weighted = join(half, parts)
            x = weighted / total
            x = jnp.concatenate([x[:, 0 : rows // 2], x[:, rows // 2 : rows]], axis=0).T
            units = x.shape[0] // heads
            for g in range(heads):
                column = (j * heads + g) * head_dim
                lhs_ref[side, :, column : column + head_dim] = x[
                    g * units : (g + 1) * units
                ].astype(jnp.bfloat16)
    own, partner = lhs_ref[0], lhs_ref[1]
    for start in range(0, width, tile):
        columns = slice(start, start + tile)
        out = jnp.dot(own, weight_ref[:, columns], preferred_element_type=jnp.float32)
        out += jnp.dot(partner, partner_ref[:, columns], preferred_element_type=jnp.float32)
        for p in range(chips):
            out_ref[p, :, columns] = out[p * few : (p + 1) * few].astype(jnp.bfloat16)


def project(parts, out_weight, partner_weight, chips, few, heads, head_dim):
    own_width, width = out_weight.shape
    tile = next(t for t in (768, 640, 512, 384, 256, 128, width) if width % t == 0)
    return pl.pallas_call(
        functools.partial(project_kernel, heads, head_dim, tile),
        out_shape=jax.ShapeDtypeStruct((chips, few, width), jnp.bfloat16),
        in_specs=[VMEM_SPEC] * 3,
        out_specs=VMEM_SPEC,
        scratch_shapes=[pltpu.VMEM((2, chips * few, own_width), jnp.bfloat16)],
        compiler_params=params(),
    )(parts, out_weight, partner_weight)


def finish_kernel(terms_ref, residual_ref, gain_ref, out_ref):
    branch = terms_ref[0].astype(jnp.float32)
    for p in range(1, terms_ref.shape[0]):
        branch += terms_ref[p].astype(jnp.float32)
    mean_square = jnp.mean(branch * branch, axis=1, keepdims=True)
    normed = branch * lax.rsqrt(mean_square + EPSILON) * gain_ref[...][None]
    out_ref[...] = residual_ref[...].astype(jnp.float32) + normed


def sublayer(n, queries, keys, values, residual, post_gain, out_weight):
    kv_heads, _, head_dim = keys.shape
    chips = n // 2
    head_count = queries.shape[1] // head_dim
    own_heads = out_weight.shape[0] // head_dim
    heads = min(head_count // kv_heads, own_heads)
    width = out_weight.shape[1]
    planes = n // 4
    same_core = [[2 * p + c for p in range(chips)] for c in range(2)]
    same_side = [
        [4 * z + 2 * y + c for z in range(planes) for c in range(2)] for y in range(2)
    ]

    def exchange(x, groups):
        return lax.all_to_all(x, "ctx", 0, 0, axis_index_groups=groups)

    def swap(x, offset):
        return lax.ppermute(x, "ctx", [(i, i ^ offset) for i in range(n)])

    def attended(offset, x, *after):
        return attend(offset, x, keys, values, own_units, own_heads, head_count, after)

    own_units = queries.shape[0]
    cover = 4000 * keys.size * keys.dtype.itemsize
    partner_queries = swap(queries, 1)
    partner_weight = swap(out_weight, 1)
    ahead = spread(fetch(queries), partner_queries, chips, out_weight.shape[0], cover)
    theirs = exchange(ahead, same_core)
    theirs = theirs.reshape(n * own_units, theirs.shape[2])
    mine = swap(theirs, 1)
    pair = swap(attended(3, theirs), 1)
    joined = combine(head_dim, attended(2, mine), pair)
    across = swap(joined, 2)
    right = attended(1, theirs, joined)
    beside = swap(right, 1)
    own = pack(head_dim, planes, attended(0, mine, right), beside, across)
    parts = exchange(own.reshape((chips,) + own.shape[2:]), same_side)
    term = project(parts, out_weight, partner_weight, chips, own_units, heads, head_dim)
    return pl.pallas_call(
        finish_kernel,
        out_shape=jax.ShapeDtypeStruct((own_units, width), jnp.float32),
        in_specs=[VMEM_SPEC] * 3,
        out_specs=VMEM_SPEC,
        compiler_params=params(),
    )(exchange(term, same_core), residual, post_gain)


def solution(mesh):
    in_specs = (
        P(("groups", "ctx"), None),
        P(None, ("groups", "ctx"), None),
        P(None, ("groups", "ctx"), None),
        P(("groups", "ctx"), None),
        P(),
        P("ctx", None),
    )
    out_specs = P(("groups", "ctx"), None)
    return jax.shard_map(
        functools.partial(sublayer, mesh.shape["ctx"]),
        mesh=mesh,
        in_specs=in_specs,
        out_specs=out_specs,
        check_vma=False,
    )
```

profile of v0, /device:TPU:0, one launch (start us, length us, event | category | flops | bytes accessed | tf_op | source)
XLA Modules:
  0.0 56.6 jit_solution(15006643266623504109)
XLA Ops:
  0.0 0.5 collective-permute-start
  0.5 0.0 collective-permute-start.5
  0.5 0.9 %shard_map.64.own_ref = bf16[4,4096]{1,0:T(4,128)(2,1)S(1)} custom-call(bf16[4,4096]{1,0:T(4,128)(2,1)} %in_ref.1), custom_call_target="tpu_custom_call" | custom-call | bytes 2097152 | tf_op jit(solution)/shard_map/pallas_call | solution.py:58
  1.4 0.0 slice-start.1
  1.5 0.0 slice-start.3
  1.5 0.1 collective-permute-done.partner_ref
  1.6 16.5 %all_to_all.15 = bf16[8,8,2048]{2,1,0:T(8,128)(2,1)S(1)} all-to-all(bf16[8,8,2048]{2,1,0:T(8,128)(2,1)S(1)} %shard_map.65), channel_id=1, replica_groups={{0,2,4,6,8,10,12,14},{1,3,5,7,9,11,13,15},{16,18,20,22,24,26,28,30},{17..., dimensions={0} | all-to-all | bytes 524288 | tf_op jit(solution)/shard_map/all_to_all | solution.py:324
  18.1 0.0 collective-permute-start.1
  18.1 0.0 slice-done
  18.1 0.0 slice-done.1
  18.1 0.0 slice-done.3
  18.1 1.7 %shard_map.67 = bf16[4,136,128]{2,1,0:T(8,128)(2,1)S(1)} custom-call(bf16[64,2048]{1,0:T(8,128)(2,1)S(1)} %bitcast.7, bf16[16,2048,128]{2,1,0:T(8,128)(2,1)S(1)} %bitcast.3, bf16[16,2048,128]{2,1,0:T(8,128)(2,1)S(1)} %bitcast.5), custom_call_target="tpu_custom_call" | custom-call | flops 536870912 | bytes 4194304 | tf_op jit(solution)/shard_map/pallas_call | solution.py:186
  19.8 0.5 collective-permute-start.2
  20.3 0.0 collective-permute-done.1.q_ref
  20.3 1.7 %shard_map.66.refs_0_ = bf16[4,136,128]{2,1,0:T(8,128)(2,1)S(1)} custom-call(bf16[64,2048]{1,0:T(8,128)(2,1)S(1)} %collective-permute-done.1.q_ref, bf16[16,2048,128]{2,1,0:T(8,128)(2,1)S(1)} %bitcast.3, bf16[16,2048,128]{2,1,0:T(8,128)(2,1)S(1)} %bitcast.5), custom_call_target="tpu_custom_call" | custom-call | flops 536870912 | bytes 4194304 | tf_op jit(solution)/shard_map/pallas_call | solution.py:186
  22.0 0.0 collective-permute-done.2.refs_1_
  22.0 0.1 shard_map.68.refs_0_
  22.1 1.7 %shard_map.69.refs_0_ = bf16[4,136,128]{2,1,0:T(8,128)(2,1)S(1)} custom-call(bf16[64,2048]{1,0:T(8,128)(2,1)S(1)} %bitcast.8, bf16[16,2048,128]{2,1,0:T(8,128)(2,1)S(1)} %bitcast.3, bf16[16,2048,128]{2,1,0:T(8,128)(2,1)S(1)} %bitcast.5, bf16[4,136,128]{2,1,0:T(8,128)(2,1)S(1)} %shard_map.68.refs_0_), custom_call_target="tpu_custom_call" | custom-call | flops 536870912 | bytes 4194304 | tf_op jit(solution)/shard_map/pallas_call | solution.py:186
  23.8 0.0 copy-start.1
  23.8 0.0 copy-start.2
  23.9 0.1 collective-permute-start.3
  23.9 1.5 %collective-permute-start.4 = (bf16[4,136,128]{2,1,0:T(8,128)(2,1)S(1)}, bf16[4,136,128]{2,1,0:T(8,128)(2,1)S(1)}, u32[]{:S(2)}, u32[]{:S(2)}) collective-permute-start(bf16[4,136,128]{2,1,0:T(8,128)(2,1)S(1)} %shard_map.68.refs_0_), channel_id=1, source_target_pairs={{0,2},{1,3},{2,0},{3,1},{4,6},{5,7},{6,4},{7,5},{8,10},{9,11},{10,... | collective-permute-start | bytes 417800 | tf_op jit(solution)/shard_map/ppermute | solution.py:327
  25.4 1.7 %shard_map.70.refs_0_ = bf16[4,136,128]{2,1,0:T(8,128)(2,1)S(1)} custom-call(bf16[64,2048]{1,0:T(8,128)(2,1)S(1)} %collective-permute-done.1.q_ref, bf16[16,2048,128]{2,1,0:T(8,128)(2,1)S(1)} %bitcast.3, bf16[16,2048,128]{2,1,0:T(8,128)(2,1)S(1)} %bitcast.5, bf16[4,136,128]{2,1,0:T(8,128)(2,1)S(1)} %shard_map.69.refs_0_), custom_call_target="tpu_custom_call" | custom-call | flops 536870912 | bytes 4194304 | tf_op jit(solution)/shard_map/pallas_call | solution.py:186
  27.1 0.0 collective-permute-done.3.refs_1_
  27.1 2.9 %collective-permute-done.4.refs_2_ = bf16[4,136,128]{2,1,0:T(8,128)(2,1)S(1)} collective-permute-done((bf16[4,136,128]{2,1,0:T(8,128)(2,1)S(1)}, bf16[4,136,128]{2,1,0:T(8,128)(2,1)S(1)}, u32[]{:S(2)}, u32[]{:S(2)}) %collective-permute-start.4) | collective-permute-done | bytes 139296 | tf_op jit(solution)/shard_map/ppermute | solution.py:327
  30.0 0.2 shard_map.71
  30.2 9.4 %all_to_all.16.part_ref = bf16[8,1,72,128]{3,2,1,0:T(8,128)(2,1)S(1)} all-to-all(bf16[8,1,72,128]{3,2,1,0:T(8,128)(2,1)S(1)} %bitcast.9), channel_id=1, replica_groups={{0,1,4,5,8,9,12,13},{2,3,6,7,10,11,14,15},{16,17,20,21,24,25,28,29},{18..., dimensions={0} | all-to-all | bytes 294912 | tf_op jit(solution)/shard_map/all_to_all | solution.py:324
  39.6 0.0 collective-permute-done.5.partner_ref
  39.6 1.2 %shard_map.72 = bf16[8,4,5376]{2,1,0:T(4,128)(2,1)S(1)} custom-call(bf16[8,1,72,128]{3,2,1,0:T(8,128)(2,1)S(1)} %all_to_all.16.part_ref, bf16[256,5376]{1,0:T(8,128)(2,1)S(1)} %copy-done, bf16[256,5376]{1,0:T(8,128)(2,1)S(1)} %collective-permute-done.5.partner_ref), custom_call_target="tpu_custom_call" | custom-call | tf_op jit(solution)/shard_map/pallas_call | solution.py:291
  40.8 15.0 %all_to_all.17.terms_ref = bf16[8,4,5376]{2,1,0:T(4,128)(2,1)S(1)} all-to-all(bf16[8,4,5376]{2,1,0:T(4,128)(2,1)S(1)} %shard_map.72), channel_id=1, replica_groups={{0,2,4,6,8,10,12,14},{1,3,5,7,9,11,13,15},{16,18,20,22,24,26,28,30},{17..., dimensions={0} | all-to-all | bytes 688128 | tf_op jit(solution)/shard_map/all_to_all | solution.py:324
  55.7 0.0 copy-done.1
  55.7 0.8 %shard_map.73 = f32[4,5376]{1,0:T(4,128)} custom-call(bf16[8,4,5376]{2,1,0:T(4,128)(2,1)S(1)} %all_to_all.17.terms_ref, bf16[4,5376]{1,0:T(4,128)(2,1)S(1)} %copy-done.1, f32[5376]{0:T(1024)S(1)} %copy-done.2), custom_call_target="tpu_custom_call" | custom-call | tf_op jit(solution)/shard_map/pallas_call | solution.py:348
  (9 shorter events, 0.0 us)
Async XLA Ops:
  0.0 1.6 %collective-permute-start = (bf16[4,4096]{1,0:T(4,128)(2,1)}, bf16[4,4096]{1,0:T(4,128)(2,1)S(1)}, u32[]{:S(2)}, u32[]{:S(2)}) collective-permute-start(bf16[4,4096]{1,0:T(4,128)(2,1)} %in_ref.1), channel_id=1, source_target_pairs={{0,1},{1,0},{2,3},{3,2},{4,5},{5,4},{6,7},{7,6},{8,9},{9,8},{10,11... | collective-permute-start | bytes 98312 | tf_op jit(solution)/shard_map/ppermute | solution.py:327
  0.5 39.1 %collective-permute-start.5 = (bf16[256,5376]{1,0:T(8,128)(2,1)}, bf16[256,5376]{1,0:T(8,128)(2,1)S(1)}, u32[]{:S(2)}, u32[]{:S(2)}) collective-permute-start(bf16[256,5376]{1,0:T(8,128)(2,1)} %weight_ref.1), channel_id=1, source_target_pairs={{0,1},{1,0},{2,3},{3,2},{4,5},{5,4},{6,7},{7,6},{8,9},{9,8},{10,11... | collective-permute-start | bytes 8257544 | tf_op jit(solution)/shard_map/ppermute | solution.py:327
  0.5 17.6 %slice-start = ((s8[8388608]{0:T(1024)(128)(4,1)}), s8[4194304]{0:T(1024)(128)(4,1)S(1)}, s32[]{:S(2)}) async-start(s8[8388608]{0:T(1024)(128)(4,1)} %bitcast.2), calls=%async_computation.3 | async-start | bytes 8388608
  0.5 17.6 %slice-start.2 = ((s8[8388608]{0:T(1024)(128)(4,1)}), s8[4194304]{0:T(1024)(128)(4,1)S(1)}, s32[]{:S(2)}) async-start(s8[8388608]{0:T(1024)(128)(4,1)} %bitcast.4), calls=%async_computation.5 | async-start | bytes 8388608
  1.4 16.6 %slice-start.1 = ((s8[8388608]{0:T(1024)(128)(4,1)}), s8[4194304]{0:T(1024)(128)(4,1)S(1)}, s32[]{:S(2)}) async-start(s8[8388608]{0:T(1024)(128)(4,1)} %bitcast.2), calls=%async_computation.4 | async-start | bytes 8388608
  1.5 16.6 %slice-start.3 = ((s8[8388608]{0:T(1024)(128)(4,1)}), s8[4194304]{0:T(1024)(128)(4,1)S(1)}, s32[]{:S(2)}) async-start(s8[8388608]{0:T(1024)(128)(4,1)} %bitcast.4), calls=%async_computation.6 | async-start | bytes 8388608
  18.1 2.3 %collective-permute-start.1 = (bf16[64,2048]{1,0:T(8,128)(2,1)S(1)}, bf16[64,2048]{1,0:T(8,128)(2,1)S(1)}, u32[]{:S(2)}, u32[]{:S(2)}) collective-permute-start(bf16[64,2048]{1,0:T(8,128)(2,1)S(1)} %bitcast.6), channel_id=1, source_target_pairs={{0,1},{1,0},{2,3},{3,2},{4,5},{5,4},{6,7},{7,6},{8,9},{9,8},{10,11... | collective-permute-start | bytes 786440 | tf_op jit(solution)/shard_map/ppermute | solution.py:327
  19.8 2.2 %collective-permute-start.2 = (bf16[4,136,128]{2,1,0:T(8,128)(2,1)S(1)}, bf16[4,136,128]{2,1,0:T(8,128)(2,1)S(1)}, u32[]{:S(2)}, u32[]{:S(2)}) collective-permute-start(bf16[4,136,128]{2,1,0:T(8,128)(2,1)S(1)} %shard_map.67), channel_id=1, source_target_pairs={{0,1},{1,0},{2,3},{3,2},{4,5},{5,4},{6,7},{7,6},{8,9},{9,8},{10,11... | collective-permute-start | bytes 417800 | tf_op jit(solution)/shard_map/ppermute | solution.py:327
  23.8 15.8 %copy-start = (bf16[256,5376]{1,0:T(8,128)(2,1)S(1)}, bf16[256,5376]{1,0:T(8,128)(2,1)}, u32[]{:S(2)}) copy-start(bf16[256,5376]{1,0:T(8,128)(2,1)} %weight_ref.1) | copy-start | bytes 8257540
  23.8 31.9 %copy-start.1 = (bf16[4,5376]{1,0:T(4,128)(2,1)S(1)}, bf16[4,5376]{1,0:T(4,128)(2,1)}, u32[]{:S(2)}) copy-start(bf16[4,5376]{1,0:T(4,128)(2,1)} %residual_ref.1) | copy-start | bytes 129028
  23.8 31.9 %copy-start.2 = (f32[5376]{0:T(1024)S(1)}, f32[5376]{0:T(1024)}, u32[]{:S(2)}) copy-start(f32[5376]{0:T(1024)} %gain_ref.1) | copy-start | bytes 64516
  23.9 3.2 %collective-permute-start.3 = (bf16[4,136,128]{2,1,0:T(8,128)(2,1)S(1)}, bf16[4,136,128]{2,1,0:T(8,128)(2,1)S(1)}, u32[]{:S(2)}, u32[]{:S(2)}) collective-permute-start(bf16[4,136,128]{2,1,0:T(8,128)(2,1)S(1)} %shard_map.69.refs_0_), channel_id=1, source_target_pairs={{0,1},{1,0},{2,3},{3,2},{4,5},{5,4},{6,7},{7,6},{8,9},{9,8},{10,11... | collective-permute-start | bytes 417800 | tf_op jit(solution)/shard_map/ppermute | solution.py:327
  23.9 6.1 %collective-permute-start.4 = (bf16[4,136,128]{2,1,0:T(8,128)(2,1)S(1)}, bf16[4,136,128]{2,1,0:T(8,128)(2,1)S(1)}, u32[]{:S(2)}, u32[]{:S(2)}) collective-permute-start(bf16[4,136,128]{2,1,0:T(8,128)(2,1)S(1)} %shard_map.68.refs_0_), channel_id=1, source_target_pairs={{0,2},{1,3},{2,0},{3,1},{4,6},{5,7},{6,4},{7,5},{8,10},{9,11},{10,... | collective-permute-start | bytes 417800 | tf_op jit(solution)/shard_map/ppermute | solution.py:327
where the time goes:
time: 56.8 us; the launch traced here: 56.6 us
  blocking collectives  40.8 us (72%)
  Pallas kernels  9.96 us (18%)
  waiting for transfers between devices  3.01 us (5%)
  starting transfers between devices  2.61 us (5%)
    all_to_all x3, blocking collectives, exchange(): return lax.all_to_all(x, 'ctx', 0, 0, axis_index_groups=groups)  40.8 us
    pallas_call x4, Pallas kernels, attend(): pl.pallas_call(functools.partial(attend_kernel, offset, few, own_heads, h...  6.74 us
    ppermute x6, waiting for transfers between devices, swap(): return lax.ppermute(x, 'ctx', [(i, i ^ offset) for i in range(n)])  3.01 us
    ppermute x6, starting transfers between devices, swap(): return lax.ppermute(x, 'ctx', [(i, i ^ offset) for i in range(n)])  2.61 us
    pallas_call x1, Pallas kernels, project(): pl.pallas_call(functools.partial(project_kernel, heads, head_dim, tile),...  1.2 us
  transfers between devices with their start and end apart: 6, of which 2 were waited for; matrix products, arithmetic and copies ran while one was open for 0% of the time, Pallas kernels for 14%

commit v1 on v0

--- a/solution.py
+++ b/solution.py
@@ -98,7 +98,7 @@
 
 
 def attend_kernel(
-    offset, few, own_heads, heads, group, head_dim, chunk, tasks,
+    offset, few, own_heads, heads, group, head_dim, chunk, tasks, span,
     q_ref, k_ref, v_ref, *refs,
 ):
     out_ref, score_a, score_b = refs[-3:]
@@ -158,44 +158,47 @@
             total = exponents if total is None else total + exponents
             weighted = product if weighted is None else weighted + product
         total = jnp.sum(total, axis=1, keepdims=True)
-        out_ref[t, 0:head_dim, :] = weighted.T.astype(jnp.bfloat16)
+        out_ref[t - span[0], 0:head_dim, :] = weighted.T.astype(jnp.bfloat16)
         lane = lax.broadcasted_iota(jnp.int32, (peak.shape[0], 128), 1)
         stats = jnp.where(lane == 0, peak, total).T
-        out_ref[t, head_dim : head_dim + AUX, :] = pack_aux(stats[0:1], stats[1:2])
+        out_ref[t - span[0], head_dim : head_dim + AUX, :] = pack_aux(stats[0:1], stats[1:2])
         return None if highest is None else jnp.max(highest, axis=1, keepdims=True)
 
-    q = load_query(0)
+    q = load_query(span[0])
     highest = None
     for start in range(0, positions, chunk):
-        part = score(q, first_head(0) // group, start, score_a)
+        part = score(q, first_head(span[0]) // group, start, score_a)
         highest = part if highest is None else jnp.maximum(highest, part)
     peak = jnp.max(highest, axis=1, keepdims=True)
 
-    for t in range(tasks):
-        score_refs = (score_a, score_b) if t % 2 == 0 else (score_b, score_a)
-        peak = section(t, peak, score_refs[0], t + 1 if t + 1 < tasks else None, score_refs[1])
-
-
-def attend(offset, queries, keys, values, few, own_heads, head_count, after):
+    for t in range(*span):
+        score_refs = (score_a, score_b) if (t - span[0]) % 2 == 0 else (score_b, score_a)
+        following = t + 1 if t + 1 < span[1] else None
+        peak = section(t, peak, score_refs[0], following, score_refs[1])
+
+
+def attend(offset, queries, keys, values, few, own_heads, head_count, part, after):
     kv_heads, positions, head_dim = keys.shape
     units = queries.shape[0]
     group = head_count // kv_heads
     heads = min(group, own_heads)
     tasks = head_count // (4 * heads)
     rows = units * heads
+    span = (0, tasks) if part is None else (part * tasks // 2, (part + 1) * tasks // 2)
+    count = span[1] - span[0]
     return pl.pallas_call(
         functools.partial(
-            attend_kernel, offset, few, own_heads, heads, group, head_dim, min(CHUNK, positions), tasks
+            attend_kernel, offset, few, own_heads, heads, group, head_dim, min(CHUNK, positions), tasks, span
         ),
-        out_shape=jax.ShapeDtypeStruct((tasks, head_dim + AUX, rows), jnp.bfloat16),
+        out_shape=jax.ShapeDtypeStruct((count, head_dim + AUX, rows), jnp.bfloat16),
         in_specs=[VMEM_SPEC] * (3 + len(after)),
         out_specs=VMEM_SPEC,
         scratch_shapes=[pltpu.VMEM((rows, positions), jnp.float32)] * 2,
         compiler_params=params(20 << 20),
         cost_estimate=pl.CostEstimate(
-            flops=4 * tasks * rows * positions * head_dim,
-            bytes_accessed=4 * tasks * positions * head_dim,
-            transcendentals=tasks * rows * positions,
+            flops=4 * count * rows * positions * head_dim,
+            bytes_accessed=4 * count * positions * head_dim,
+            transcendentals=count * rows * positions,
         ),
     )(queries, keys, values, *after)
 
@@ -211,30 +214,31 @@
     return peak, total, functools.reduce(jnp.add, weighted)
 
 
-def combine_kernel(head_dim, *refs):
-    out_ref = refs[-1]
+def combine_kernel(head_dim, first, half_ref, whole_ref, out_ref):
     for t in range(out_ref.shape[0]):
-        peak, total, weighted = join(head_dim, [ref.at[t] for ref in refs[:-1]])
+        parts = [half_ref.at[t], whole_ref.at[first + t]]
+        peak, total, weighted = join(head_dim, parts)
         out_ref[t, 0:head_dim, :] = weighted.astype(jnp.bfloat16)
         out_ref[t, head_dim : head_dim + AUX, :] = pack_aux(peak, total)
 
 
-def combine(head_dim, *parts):
-    return pl.pallas_call(
-        functools.partial(combine_kernel, head_dim),
-        out_shape=jax.ShapeDtypeStruct(parts[0].shape, jnp.bfloat16),
-        in_specs=[VMEM_SPEC] * len(parts),
+def combine(head_dim, first, half, whole):
+    return pl.pallas_call(
+        functools.partial(combine_kernel, head_dim, first),
+        out_shape=jax.ShapeDtypeStruct(half.shape, jnp.bfloat16),
+        in_specs=[VMEM_SPEC] * 2,
         out_specs=VMEM_SPEC,
         compiler_params=params(),
-    )(*parts)
-
-
-def pack_kernel(head_dim, *refs):
-    out_ref = refs[-1]
+    )(half, whole)
+
+
+def pack_kernel(head_dim, own_ref, beside_ref, first_ref, second_ref, out_ref):
     per_device = out_ref.shape[2]
     half = head_dim // 2
-    for t in range(refs[0].shape[0]):
-        peak, total, weighted = join(head_dim, [ref.at[t] for ref in refs[:-1]])
+    early = first_ref.shape[0]
+    for t in range(own_ref.shape[0]):
+        across = first_ref.at[t] if t < early else second_ref.at[t - early]
+        peak, total, weighted = join(head_dim, [own_ref.at[t], beside_ref.at[t], across])
         aux = pack_aux(peak, total).astype(jnp.float32)
         units = aux.shape[1] // 2
         for core in range(2):
@@ -326,8 +330,10 @@
     def swap(x, offset):
         return lax.ppermute(x, "ctx", [(i, i ^ offset) for i in range(n)])
 
-    def attended(offset, x, *after):
-        return attend(offset, x, keys, values, own_units, own_heads, head_count, after)
+    def attended(offset, x, *after, part=None):
+        return attend(
+            offset, x, keys, values, own_units, own_heads, head_count, part, after
+        )
 
     own_units = queries.shape[0]
     cover = 4000 * keys.size * keys.dtype.itemsize
@@ -338,11 +344,15 @@
     theirs = theirs.reshape(n * own_units, theirs.shape[2])
     mine = swap(theirs, 1)
     pair = swap(attended(3, theirs), 1)
-    joined = combine(head_dim, attended(2, mine), pair)
-    across = swap(joined, 2)
-    right = attended(1, theirs, joined)
+    early = attended(2, mine, part=0)
+    first = combine(head_dim, 0, early, pair)
+    across = [swap(first, 2)]
+    late = attended(2, mine, first, part=1)
+    second = combine(head_dim, early.shape[0], late, pair)
+    across.append(swap(second, 2))
+    right = attended(1, theirs, second)
     beside = swap(right, 1)
-    own = pack(head_dim, planes, attended(0, mine, right), beside, across)
+    own = pack(head_dim, planes, attended(0, mine, right), beside, *across)
     parts = exchange(own.reshape((chips,) + own.shape[2:]), same_side)
     term = project(parts, out_weight, partner_weight, chips, own_units, heads, head_dim)
     return pl.pallas_call(

time: 56.8 us -> 57.2 us (level)
  starting transfers between devices: 2.61 us -> 3.45 us
  waiting for transfers between devices: 3.01 us -> 2.2 us
    ppermute x6 -> x7, starting transfers between devices: 2.61 us -> 3.45 us  [swap(): return lax.ppermute(x, 'ctx', [(i, i ^ offset) for i in range(n)])]
    ppermute x6 -> x7, waiting for transfers between devices: 3.01 us -> 2.2 us  [swap(): return lax.ppermute(x, 'ctx', [(i, i ^ offset) for i in range(n)])]
    pallas_call x4 -> x5, Pallas kernels: 6.74 us -> 7.13 us  [attend(): pl.pallas_call(functools.partial(attend_kernel, offset, few, own_heads, h...]
  transfers between devices with their start and end apart: 6 -> 7, of which waited for: 2 -> 3; matrix products, arithmetic and copies ran while one was open for 0% -> 0% of each run, Pallas kernels for 14% -> 15%
where the time goes in v1:
time: 57.2 us; the launch traced here: 57 us
  blocking collectives  40.8 us (71%)
  Pallas kernels  10.4 us (18%)
  starting transfers between devices  3.45 us (6%)
  waiting for transfers between devices  2.2 us (4%)
    all_to_all x3, blocking collectives, exchange(): return lax.all_to_all(x, 'ctx', 0, 0, axis_index_groups=groups)  40.8 us
    pallas_call x5, Pallas kernels, attend(): pl.pallas_call(functools.partial(attend_kernel, offset, few, own_heads, h...  7.13 us
    ppermute x7, starting transfers between devices, swap(): return lax.ppermute(x, 'ctx', [(i, i ^ offset) for i in range(n)])  3.45 us
    ppermute x7, waiting for transfers between devices, swap(): return lax.ppermute(x, 'ctx', [(i, i ^ offset) for i in range(n)])  2.2 us
    pallas_call x1, Pallas kernels, project(): pl.pallas_call(functools.partial(project_kernel, heads, head_dim, tile),...  1.2 us
  transfers between devices with their start and end apart: 7, of which 3 were waited for; matrix products, arithmetic and copies ran while one was open for 0% of the time, Pallas kernels for 15%

profile of v1, /device:TPU:0, one launch (start us, length us, event | category | flops | bytes accessed | tf_op | source)
XLA Modules:
  0.0 57.0 jit_solution(13543601893358847838)
XLA Ops:
  0.0 0.5 collective-permute-start
  0.5 0.0 collective-permute-start.6
  0.5 0.9 %shard_map.64.own_ref = bf16[4,4096]{1,0:T(4,128)(2,1)S(1)} custom-call(bf16[4,4096]{1,0:T(4,128)(2,1)} %in_ref.1), custom_call_target="tpu_custom_call" | custom-call | bytes 2097152 | tf_op jit(solution)/shard_map/pallas_call | solution.py:58
  1.4 0.0 slice-start.1
  1.5 0.0 slice-start.3
  1.5 0.1 collective-permute-done.partner_ref
  1.6 16.5 %all_to_all.15 = bf16[8,8,2048]{2,1,0:T(8,128)(2,1)S(1)} all-to-all(bf16[8,8,2048]{2,1,0:T(8,128)(2,1)S(1)} %shard_map.65), channel_id=1, replica_groups={{0,2,4,6,8,10,12,14},{1,3,5,7,9,11,13,15},{16,18,20,22,24,26,28,30},{17..., dimensions={0} | all-to-all | bytes 524288 | tf_op jit(solution)/shard_map/all_to_all | solution.py:328
  18.1 0.0 collective-permute-start.1
  18.1 1.7 %shard_map.67 = bf16[4,136,128]{2,1,0:T(8,128)(2,1)S(1)} custom-call(bf16[64,2048]{1,0:T(8,128)(2,1)S(1)} %bitcast.7, bf16[16,2048,128]{2,1,0:T(8,128)(2,1)S(1)} %bitcast.3, bf16[16,2048,128]{2,1,0:T(8,128)(2,1)S(1)} %bitcast.5), custom_call_target="tpu_custom_call" | custom-call | flops 536870912 | bytes 4194304 | tf_op jit(solution)/shard_map/pallas_call | solution.py:189
  19.8 0.5 collective-permute-start.2
  20.3 0.0 collective-permute-done.1.q_ref
  20.3 1.0 %shard_map.66.half_ref = bf16[2,136,128]{2,1,0:T(8,128)(2,1)S(1)} custom-call(bf16[64,2048]{1,0:T(8,128)(2,1)S(1)} %collective-permute-done.1.q_ref, bf16[16,2048,128]{2,1,0:T(8,128)(2,1)S(1)} %bitcast.3, bf16[16,2048,128]{2,1,0:T(8,128)(2,1)S(1)} %bitcast.5), custom_call_target="tpu_custom_call" | custom-call | flops 268435456 | bytes 2097152 | tf_op jit(solution)/shard_map/pallas_call | solution.py:189
  21.4 0.0 collective-permute-done.2.whole_ref
  21.4 0.1 shard_map.68.refs_0_
  21.5 1.0 %shard_map.69.half_ref = bf16[2,136,128]{2,1,0:T(8,128)(2,1)S(1)} custom-call(bf16[64,2048]{1,0:T(8,128)(2,1)S(1)} %collective-permute-done.1.q_ref, bf16[16,2048,128]{2,1,0:T(8,128)(2,1)S(1)} %bitcast.3, bf16[16,2048,128]{2,1,0:T(8,128)(2,1)S(1)} %bitcast.5, bf16[2,136,128]{2,1,0:T(8,128)(2,1)S(1)} %shard_map.68.refs_0_), custom_call_target="tpu_custom_call" | custom-call | flops 268435456 | bytes 2097152 | tf_op jit(solution)/shard_map/pallas_call | solution.py:189
  22.5 0.1 shard_map.70.refs_0_
  22.6 1.7 %shard_map.71.refs_0_ = bf16[4,136,128]{2,1,0:T(8,128)(2,1)S(1)} custom-call(bf16[64,2048]{1,0:T(8,128)(2,1)S(1)} %bitcast.8, bf16[16,2048,128]{2,1,0:T(8,128)(2,1)S(1)} %bitcast.3, bf16[16,2048,128]{2,1,0:T(8,128)(2,1)S(1)} %bitcast.5, bf16[2,136,128]{2,1,0:T(8,128)(2,1)S(1)} %shard_map.70.refs_0_), custom_call_target="tpu_custom_call" | custom-call | flops 536870912 | bytes 4194304 | tf_op jit(solution)/shard_map/pallas_call | solution.py:189
  24.3 0.0 copy-start.1
  24.3 0.0 copy-start.2
  24.3 0.4 collective-permute-start.3
  24.6 1.4 %collective-permute-start.5 = (bf16[2,136,128]{2,1,0:T(8,128)(2,1)S(1)}, bf16[2,136,128]{2,1,0:T(8,128)(2,1)S(1)}, u32[]{:S(2)}, u32[]{:S(2)}) collective-permute-start(bf16[2,136,128]{2,1,0:T(8,128)(2,1)S(1)} %shard_map.70.refs_0_), channel_id=1, source_target_pairs={{0,2},{1,3},{2,0},{3,1},{4,6},{5,7},{6,4},{7,5},{8,10},{9,11},{10,... | collective-permute-start | bytes 208904 | tf_op jit(solution)/shard_map/ppermute | solution.py:331
  26.1 0.6 %collective-permute-start.4 = (bf16[2,136,128]{2,1,0:T(8,128)(2,1)S(1)}, bf16[2,136,128]{2,1,0:T(8,128)(2,1)S(1)}, u32[]{:S(2)}, u32[]{:S(2)}) collective-permute-start(bf16[2,136,128]{2,1,0:T(8,128)(2,1)S(1)} %shard_map.68.refs_0_), channel_id=1, source_target_pairs={{0,2},{1,3},{2,0},{3,1},{4,6},{5,7},{6,4},{7,5},{8,10},{9,11},{10,... | collective-permute-start | bytes 208904 | tf_op jit(solution)/shard_map/ppermute | solution.py:331
  26.7 1.7 %shard_map.72.own_ref = bf16[4,136,128]{2,1,0:T(8,128)(2,1)S(1)} custom-call(bf16[64,2048]{1,0:T(8,128)(2,1)S(1)} %collective-permute-done.1.q_ref, bf16[16,2048,128]{2,1,0:T(8,128)(2,1)S(1)} %bitcast.3, bf16[16,2048,128]{2,1,0:T(8,128)(2,1)S(1)} %bitcast.5, bf16[4,136,128]{2,1,0:T(8,128)(2,1)S(1)} %shard_map.71.refs_0_), custom_call_target="tpu_custom_call" | custom-call | flops 536870912 | bytes 4194304 | tf_op jit(solution)/shard_map/pallas_call | solution.py:189
  28.4 1.0 %collective-permute-done.5.second_ref = bf16[2,136,128]{2,1,0:T(8,128)(2,1)S(1)} collective-permute-done((bf16[2,136,128]{2,1,0:T(8,128)(2,1)S(1)}, bf16[2,136,128]{2,1,0:T(8,128)(2,1)S(1)}, u32[]{:S(2)}, u32[]{:S(2)}) %collective-permute-start.5) | collective-permute-done | bytes 69664 | tf_op jit(solution)/shard_map/ppermute | solution.py:331
  29.3 1.1 %collective-permute-done.4.first_ref = bf16[2,136,128]{2,1,0:T(8,128)(2,1)S(1)} collective-permute-done((bf16[2,136,128]{2,1,0:T(8,128)(2,1)S(1)}, bf16[2,136,128]{2,1,0:T(8,128)(2,1)S(1)}, u32[]{:S(2)}, u32[]{:S(2)}) %collective-permute-start.4) | collective-permute-done | bytes 69664 | tf_op jit(solution)/shard_map/ppermute | solution.py:331
  30.4 0.0 collective-permute-done.3.beside_ref
  30.4 0.2 shard_map.73
  30.6 9.4 %all_to_all.16.part_ref = bf16[8,1,72,128]{3,2,1,0:T(8,128)(2,1)S(1)} all-to-all(bf16[8,1,72,128]{3,2,1,0:T(8,128)(2,1)S(1)} %bitcast.9), channel_id=1, replica_groups={{0,1,4,5,8,9,12,13},{2,3,6,7,10,11,14,15},{16,17,20,21,24,25,28,29},{18..., dimensions={0} | all-to-all | bytes 294912 | tf_op jit(solution)/shard_map/all_to_all | solution.py:328
  40.1 0.0 collective-permute-done.6.partner_ref
  40.1 1.2 %shard_map.74 = bf16[8,4,5376]{2,1,0:T(4,128)(2,1)S(1)} custom-call(bf16[8,1,72,128]{3,2,1,0:T(8,128)(2,1)S(1)} %all_to_all.16.part_ref, bf16[256,5376]{1,0:T(8,128)(2,1)S(1)} %copy-done, bf16[256,5376]{1,0:T(8,128)(2,1)S(1)} %collective-permute-done.6.partner_ref), custom_call_target="tpu_custom_call" | custom-call | tf_op jit(solution)/shard_map/pallas_call | solution.py:295
  41.3 14.9 %all_to_all.17.terms_ref = bf16[8,4,5376]{2,1,0:T(4,128)(2,1)S(1)} all-to-all(bf16[8,4,5376]{2,1,0:T(4,128)(2,1)S(1)} %shard_map.74), channel_id=1, replica_groups={{0,2,4,6,8,10,12,14},{1,3,5,7,9,11,13,15},{16,18,20,22,24,26,28,30},{17..., dimensions={0} | all-to-all | bytes 688128 | tf_op jit(solution)/shard_map/all_to_all | solution.py:328
  56.2 0.8 %shard_map.75 = f32[4,5376]{1,0:T(4,128)} custom-call(bf16[8,4,5376]{2,1,0:T(4,128)(2,1)S(1)} %all_to_all.17.terms_ref, bf16[4,5376]{1,0:T(4,128)(2,1)S(1)} %copy-done.1, f32[5376]{0:T(1024)S(1)} %copy-done.2), custom_call_target="tpu_custom_call" | custom-call | tf_op jit(solution)/shard_map/pallas_call | solution.py:358
  (13 shorter events, 0.0 us)
Async XLA Ops:
  0.0 1.6 %collective-permute-start = (bf16[4,4096]{1,0:T(4,128)(2,1)}, bf16[4,4096]{1,0:T(4,128)(2,1)S(1)}, u32[]{:S(2)}, u32[]{:S(2)}) collective-permute-start(bf16[4,4096]{1,0:T(4,128)(2,1)} %in_ref.1), channel_id=1, source_target_pairs={{0,1},{1,0},{2,3},{3,2},{4,5},{5,4},{6,7},{7,6},{8,9},{9,8},{10,11... | collective-permute-start | bytes 98312 | tf_op jit(solution)/shard_map/ppermute | solution.py:331
  0.5 39.6 %collective-permute-start.6 = (bf16[256,5376]{1,0:T(8,128)(2,1)}, bf16[256,5376]{1,0:T(8,128)(2,1)S(1)}, u32[]{:S(2)}, u32[]{:S(2)}) collective-permute-start(bf16[256,5376]{1,0:T(8,128)(2,1)} %weight_ref.1), channel_id=1, source_target_pairs={{0,1},{1,0},{2,3},{3,2},{4,5},{5,4},{6,7},{7,6},{8,9},{9,8},{10,11... | collective-permute-start | bytes 8257544 | tf_op jit(solution)/shard_map/ppermute | solution.py:331
  0.5 17.6 %slice-start = ((s8[8388608]{0:T(1024)(128)(4,1)}), s8[4194304]{0:T(1024)(128)(4,1)S(1)}, s32[]{:S(2)}) async-start(s8[8388608]{0:T(1024)(128)(4,1)} %bitcast.2), calls=%async_computation.3 | async-start | bytes 8388608
  0.5 17.6 %slice-start.2 = ((s8[8388608]{0:T(1024)(128)(4,1)}), s8[4194304]{0:T(1024)(128)(4,1)S(1)}, s32[]{:S(2)}) async-start(s8[8388608]{0:T(1024)(128)(4,1)} %bitcast.4), calls=%async_computation.5 | async-start | bytes 8388608
  1.4 16.6 %slice-start.1 = ((s8[8388608]{0:T(1024)(128)(4,1)}), s8[4194304]{0:T(1024)(128)(4,1)S(1)}, s32[]{:S(2)}) async-start(s8[8388608]{0:T(1024)(128)(4,1)} %bitcast.2), calls=%async_computation.4 | async-start | bytes 8388608
  1.5 16.6 %slice-start.3 = ((s8[8388608]{0:T(1024)(128)(4,1)}), s8[4194304]{0:T(1024)(128)(4,1)S(1)}, s32[]{:S(2)}) async-start(s8[8388608]{0:T(1024)(128)(4,1)} %bitcast.4), calls=%async_computation.6 | async-start | bytes 8388608
  18.1 2.3 %collective-permute-start.1 = (bf16[64,2048]{1,0:T(8,128)(2,1)S(1)}, bf16[64,2048]{1,0:T(8,128)(2,1)S(1)}, u32[]{:S(2)}, u32[]{:S(2)}) collective-permute-start(bf16[64,2048]{1,0:T(8,128)(2,1)S(1)} %bitcast.6), channel_id=1, source_target_pairs={{0,1},{1,0},{2,3},{3,2},{4,5},{5,4},{6,7},{7,6},{8,9},{9,8},{10,11... | collective-permute-start | bytes 786440 | tf_op jit(solution)/shard_map/ppermute | solution.py:331
  19.8 1.6 %collective-permute-start.2 = (bf16[4,136,128]{2,1,0:T(8,128)(2,1)S(1)}, bf16[4,136,128]{2,1,0:T(8,128)(2,1)S(1)}, u32[]{:S(2)}, u32[]{:S(2)}) collective-permute-start(bf16[4,136,128]{2,1,0:T(8,128)(2,1)S(1)} %shard_map.67), channel_id=1, source_target_pairs={{0,1},{1,0},{2,3},{3,2},{4,5},{5,4},{6,7},{7,6},{8,9},{9,8},{10,11... | collective-permute-start | bytes 417800 | tf_op jit(solution)/shard_map/ppermute | solution.py:331
  24.2 15.8 %copy-start = (bf16[256,5376]{1,0:T(8,128)(2,1)S(1)}, bf16[256,5376]{1,0:T(8,128)(2,1)}, u32[]{:S(2)}) copy-start(bf16[256,5376]{1,0:T(8,128)(2,1)} %weight_ref.1) | copy-start | bytes 8257540
  24.3 31.9 %copy-start.1 = (bf16[4,5376]{1,0:T(4,128)(2,1)S(1)}, bf16[4,5376]{1,0:T(4,128)(2,1)}, u32[]{:S(2)}) copy-start(bf16[4,5376]{1,0:T(4,128)(2,1)} %residual_ref.1) | copy-start | bytes 129028
  24.3 31.9 %copy-start.2 = (f32[5376]{0:T(1024)S(1)}, f32[5376]{0:T(1024)}, u32[]{:S(2)}) copy-start(f32[5376]{0:T(1024)} %gain_ref.1) | copy-start | bytes 64516
  24.3 6.2 %collective-permute-start.3 = (bf16[4,136,128]{2,1,0:T(8,128)(2,1)S(1)}, bf16[4,136,128]{2,1,0:T(8,128)(2,1)S(1)}, u32[]{:S(2)}, u32[]{:S(2)}) collective-permute-start(bf16[4,136,128]{2,1,0:T(8,128)(2,1)S(1)} %shard_map.71.refs_0_), channel_id=1, source_target_pairs={{0,1},{1,0},{2,3},{3,2},{4,5},{5,4},{6,7},{7,6},{8,9},{9,8},{10,11... | collective-permute-start | bytes 417800 | tf_op jit(solution)/shard_map/ppermute | solution.py:331
  24.6 4.7 %collective-permute-start.5 = (bf16[2,136,128]{2,1,0:T(8,128)(2,1)S(1)}, bf16[2,136,128]{2,1,0:T(8,128)(2,1)S(1)}, u32[]{:S(2)}, u32[]{:S(2)}) collective-permute-start(bf16[2,136,128]{2,1,0:T(8,128)(2,1)S(1)} %shard_map.70.refs_0_), channel_id=1, source_target_pairs={{0,2},{1,3},{2,0},{3,1},{4,6},{5,7},{6,4},{7,5},{8,10},{9,11},{10,... | collective-permute-start | bytes 208904 | tf_op jit(solution)/shard_map/ppermute | solution.py:331
  26.1 4.4 %collective-permute-start.4 = (bf16[2,136,128]{2,1,0:T(8,128)(2,1)S(1)}, bf16[2,136,128]{2,1,0:T(8,128)(2,1)S(1)}, u32[]{:S(2)}, u32[]{:S(2)}) collective-permute-start(bf16[2,136,128]{2,1,0:T(8,128)(2,1)S(1)} %shard_map.68.refs_0_), channel_id=1, source_target_pairs={{0,2},{1,3},{2,0},{3,1},{4,6},{5,7},{6,4},{7,5},{8,10},{9,11},{10,... | collective-permute-start | bytes 208904 | tf_op jit(solution)/shard_map/ppermute | solution.py:331

commit v2 on v0

--- a/solution.py
+++ b/solution.py
@@ -98,20 +98,23 @@
 
 
 def attend_kernel(
-    offset, few, own_heads, heads, group, head_dim, chunk, tasks,
-    q_ref, k_ref, v_ref, *refs,
+    offsets, few, own_heads, heads, group, head_dim, chunk, tasks,
+    k_ref, v_ref, *refs,
 ):
-    out_ref, score_a, score_b = refs[-3:]
+    q_refs, (out_ref, score_a, score_b) = refs[: len(offsets)], refs[-3:]
     positions = k_ref.shape[1]
     per_device = own_heads // heads
-    slot = slot_of(offset)
-
-    def first_head(t):
-        device = 4 * (t // per_device) + slot
+    slots = [slot_of(offset) for offset in offsets]
+
+    def first_head(item):
+        call, t = divmod(item, tasks)
+        device = 4 * (t // per_device) + slots[call]
         return device * own_heads + (t % per_device) * heads
 
-    def load_query(t):
-        first = t * heads + (0 if offset >= 2 else tasks * heads)
+    def load_query(item):
+        call, t = divmod(item, tasks)
+        q_ref = q_refs[call]
+        first = t * heads + (0 if offsets[call] >= 2 else tasks * heads)
         columns = [
             q_ref[:, (first + g) * head_dim : (first + g + 1) * head_dim].astype(jnp.float32)
             for g in range(heads)
@@ -171,33 +174,35 @@
         highest = part if highest is None else jnp.maximum(highest, part)
     peak = jnp.max(highest, axis=1, keepdims=True)
 
-    for t in range(tasks):
+    count = len(offsets) * tasks
+    for t in range(count):
         score_refs = (score_a, score_b) if t % 2 == 0 else (score_b, score_a)
-        peak = section(t, peak, score_refs[0], t + 1 if t + 1 < tasks else None, score_refs[1])
-
-
-def attend(offset, queries, keys, values, few, own_heads, head_count, after):
+        peak = section(t, peak, score_refs[0], t + 1 if t + 1 < count else None, score_refs[1])
+
+
+def attend(offsets, queries, keys, values, few, own_heads, head_count, after):
     kv_heads, positions, head_dim = keys.shape
-    units = queries.shape[0]
+    units = queries[0].shape[0]
     group = head_count // kv_heads
     heads = min(group, own_heads)
     tasks = head_count // (4 * heads)
     rows = units * heads
+    count = len(offsets) * tasks
     return pl.pallas_call(
         functools.partial(
-            attend_kernel, offset, few, own_heads, heads, group, head_dim, min(CHUNK, positions), tasks
+            attend_kernel, offsets, few, own_heads, heads, group, head_dim, min(CHUNK, positions), tasks
         ),
-        out_shape=jax.ShapeDtypeStruct((tasks, head_dim + AUX, rows), jnp.bfloat16),
-        in_specs=[VMEM_SPEC] * (3 + len(after)),
+        out_shape=jax.ShapeDtypeStruct((count, head_dim + AUX, rows), jnp.bfloat16),
+        in_specs=[VMEM_SPEC] * (2 + len(offsets) + len(after)),
         out_specs=VMEM_SPEC,
         scratch_shapes=[pltpu.VMEM((rows, positions), jnp.float32)] * 2,
         compiler_params=params(20 << 20),
         cost_estimate=pl.CostEstimate(
-            flops=4 * tasks * rows * positions * head_dim,
-            bytes_accessed=4 * tasks * positions * head_dim,
-            transcendentals=tasks * rows * positions,
+            flops=4 * count * rows * positions * head_dim,
+            bytes_accessed=4 * count * positions * head_dim,
+            transcendentals=count * rows * positions,
         ),
-    )(queries, keys, values, *after)
+    )(keys, values, *queries, *after)
 
 
 def join(head_dim, parts):
@@ -233,8 +238,11 @@
     out_ref = refs[-1]
     per_device = out_ref.shape[2]
     half = head_dim // 2
-    for t in range(refs[0].shape[0]):
-        peak, total, weighted = join(head_dim, [ref.at[t] for ref in refs[:-1]])
+    both_ref, others = refs[0], refs[1:-1]
+    tasks = others[0].shape[0]
+    for t in range(tasks):
+        parts = [both_ref.at[tasks + t]] + [ref.at[t] for ref in others]
+        peak, total, weighted = join(head_dim, parts)
         aux = pack_aux(peak, total).astype(jnp.float32)
         units = aux.shape[1] // 2
         for core in range(2):
@@ -247,7 +255,7 @@
 
 
 def pack(head_dim, planes, *parts):
-    tasks, _, rows = parts[0].shape
+    tasks, _, rows = parts[1].shape
     shape = (planes, 2, tasks // planes, head_dim // 2 + AUX, rows)
     return pl.pallas_call(
         functools.partial(pack_kernel, head_dim),
@@ -326,8 +334,8 @@
     def swap(x, offset):
         return lax.ppermute(x, "ctx", [(i, i ^ offset) for i in range(n)])
 
-    def attended(offset, x, *after):
-        return attend(offset, x, keys, values, own_units, own_heads, head_count, after)
+    def attended(offsets, x, *after):
+        return attend(offsets, x, keys, values, own_units, own_heads, head_count, after)
 
     own_units = queries.shape[0]
     cover = 4000 * keys.size * keys.dtype.itemsize
@@ -337,12 +345,12 @@
     theirs = exchange(ahead, same_core)
     theirs = theirs.reshape(n * own_units, theirs.shape[2])
     mine = swap(theirs, 1)
-    pair = swap(attended(3, theirs), 1)
-    joined = combine(head_dim, attended(2, mine), pair)
+    pair = swap(attended((3,), (theirs,)), 1)
+    joined = combine(head_dim, attended((2,), (mine,)), pair)
     across = swap(joined, 2)
-    right = attended(1, theirs, joined)
-    beside = swap(right, 1)
-    own = pack(head_dim, planes, attended(0, mine, right), beside, across)
+    both = attended((1, 0), (theirs, mine), joined)
+    beside = swap(both[: both.shape[0] // 2], 1)
+    own = pack(head_dim, planes, both, beside, across)
     parts = exchange(own.reshape((chips,) + own.shape[2:]), same_side)
     term = project(parts, out_weight, partner_weight, chips, own_units, heads, head_dim)
     return pl.pallas_call(

time: 56.8 us -> 58.1 us (1.023)
  waiting for transfers between devices: 3.01 us -> 4.7 us
    ppermute x6, waiting for transfers between devices: 3.01 us -> 4.7 us  [swap(): return lax.ppermute(x, 'ctx', [(i, i ^ offset) for i in range(n)])]
    pallas_call x4 -> x3, Pallas kernels: 6.74 us -> 6.39 us  [attend(): pl.pallas_call(functools.partial(attend_kernel, offsets, few, own_heads,...]
  transfers between devices with their start and end apart: 6 -> 6, of which waited for: 2 -> 2; matrix products, arithmetic and copies ran while one was open for 0% -> 0% of each run, Pallas kernels for 14% -> 13%
where the time goes in v2:
time: 58.1 us; the launch traced here: 57.9 us
  blocking collectives  40.8 us (70%)
  Pallas kernels  9.62 us (17%)
  waiting for transfers between devices  4.7 us (8%)
  starting transfers between devices  2.62 us (5%)
    all_to_all x3, blocking collectives, exchange(): return lax.all_to_all(x, 'ctx', 0, 0, axis_index_groups=groups)  40.8 us
    pallas_call x3, Pallas kernels, attend(): pl.pallas_call(functools.partial(attend_kernel, offsets, few, own_heads,...  6.39 us
    ppermute x6, waiting for transfers between devices, swap(): return lax.ppermute(x, 'ctx', [(i, i ^ offset) for i in range(n)])  4.7 us
    ppermute x6, starting transfers between devices, swap(): return lax.ppermute(x, 'ctx', [(i, i ^ offset) for i in range(n)])  2.62 us
    pallas_call x1, Pallas kernels, project(): pl.pallas_call(functools.partial(project_kernel, heads, head_dim, tile),...  1.2 us
  transfers between devices with their start and end apart: 6, of which 2 were waited for; matrix products, arithmetic and copies ran while one was open for 0% of the time, Pallas kernels for 13%

profile of v2, /device:TPU:0, one launch (start us, length us, event | category | flops | bytes accessed | tf_op | source)
XLA Modules:
  0.0 57.9 jit_solution(3519435714524050404)
XLA Ops:
  0.0 0.5 collective-permute-start
  0.5 0.0 collective-permute-start.5
  0.5 0.9 %shard_map.64.own_ref = bf16[4,4096]{1,0:T(4,128)(2,1)S(1)} custom-call(bf16[4,4096]{1,0:T(4,128)(2,1)} %in_ref.1), custom_call_target="tpu_custom_call" | custom-call | bytes 2097152 | tf_op jit(solution)/shard_map/pallas_call | solution.py:58
  1.4 0.0 slice-start.1
  1.5 0.0 slice-start.3
  1.5 0.1 collective-permute-done.partner_ref
  1.6 16.5 %all_to_all.15 = bf16[8,8,2048]{2,1,0:T(8,128)(2,1)S(1)} all-to-all(bf16[8,8,2048]{2,1,0:T(8,128)(2,1)S(1)} %shard_map.65), channel_id=1, replica_groups={{0,2,4,6,8,10,12,14},{1,3,5,7,9,11,13,15},{16,18,20,22,24,26,28,30},{17..., dimensions={0} | all-to-all | bytes 524288 | tf_op jit(solution)/shard_map/all_to_all | solution.py:332
  18.1 0.0 collective-permute-start.1
  18.1 0.0 slice-done.1
  18.1 0.0 slice-done.3
  18.1 1.7 %shard_map.67 = bf16[4,136,128]{2,1,0:T(8,128)(2,1)S(1)} custom-call(bf16[16,2048,128]{2,1,0:T(8,128)(2,1)S(1)} %bitcast.3, bf16[16,2048,128]{2,1,0:T(8,128)(2,1)S(1)} %bitcast.5, bf16[64,2048]{1,0:T(8,128)(2,1)S(1)} %bitcast.7), custom_call_target="tpu_custom_call" | custom-call | flops 536870912 | bytes 4194304 | tf_op jit(solution)/shard_map/pallas_call | solution.py:191
  19.8 0.5 collective-permute-start.2
  20.4 0.0 collective-permute-done.1.refs_0_.refs_1_
  20.4 1.7 %shard_map.66.refs_0_ = bf16[4,136,128]{2,1,0:T(8,128)(2,1)S(1)} custom-call(bf16[16,2048,128]{2,1,0:T(8,128)(2,1)S(1)} %bitcast.3, bf16[16,2048,128]{2,1,0:T(8,128)(2,1)S(1)} %bitcast.5, bf16[64,2048]{1,0:T(8,128)(2,1)S(1)} %collective-permute-done.1.refs_0_.refs_1_), custom_call_target="tpu_custom_call" | custom-call | flops 536870912 | bytes 4194304 | tf_op jit(solution)/shard_map/pallas_call | solution.py:191
  22.1 0.0 collective-permute-done.2.refs_1_
  22.1 0.1 shard_map.68.refs_2_
  22.2 0.0 copy-start
  22.2 0.0 copy-start.1
  22.2 0.0 copy-start.2
  22.2 3.0 %shard_map.69.refs_0_ = bf16[8,136,128]{2,1,0:T(8,128)(2,1)S(1)} custom-call(bf16[16,2048,128]{2,1,0:T(8,128)(2,1)S(1)} %bitcast.3, bf16[16,2048,128]{2,1,0:T(8,128)(2,1)S(1)} %bitcast.5, bf16[64,2048]{1,0:T(8,128)(2,1)S(1)} %bitcast.8, bf16[64,2048]{1,0:T(8,128)(2,1)S(1)} %collective-permute-done.1.refs_0_.refs_1_, bf16[4,136,128]{2,1,0:T(8,128)(2,1)S(1)} %shard_map.68.refs_2_), custom_call_target="tpu_custom_call" | custom-call | flops 1073741824 | bytes 8388608 | tf_op jit(solution)/shard_map/pallas_call | solution.py:191
  25.2 0.1 collective-permute-start.3
  25.3 1.5 %collective-permute-start.4 = (bf16[4,136,128]{2,1,0:T(8,128)(2,1)S(1)}, bf16[4,136,128]{2,1,0:T(8,128)(2,1)S(1)}, u32[]{:S(2)}, u32[]{:S(2)}) collective-permute-start(bf16[4,136,128]{2,1,0:T(8,128)(2,1)S(1)} %shard_map.68.refs_2_), channel_id=1, source_target_pairs={{0,2},{1,3},{2,0},{3,1},{4,6},{5,7},{6,4},{7,5},{8,10},{9,11},{10,... | collective-permute-start | bytes 417800 | tf_op jit(solution)/shard_map/ppermute | solution.py:335
  26.8 0.0 collective-permute-done.3.refs_1_
  26.8 4.6 %collective-permute-done.4.refs_2_ = bf16[4,136,128]{2,1,0:T(8,128)(2,1)S(1)} collective-permute-done((bf16[4,136,128]{2,1,0:T(8,128)(2,1)S(1)}, bf16[4,136,128]{2,1,0:T(8,128)(2,1)S(1)}, u32[]{:S(2)}, u32[]{:S(2)}) %collective-permute-start.4) | collective-permute-done | bytes 139296 | tf_op jit(solution)/shard_map/ppermute | solution.py:335
  31.4 0.2 shard_map.70
  31.6 9.4 %all_to_all.16.part_ref = bf16[8,1,72,128]{3,2,1,0:T(8,128)(2,1)S(1)} all-to-all(bf16[8,1,72,128]{3,2,1,0:T(8,128)(2,1)S(1)} %bitcast.9), channel_id=1, replica_groups={{0,1,4,5,8,9,12,13},{2,3,6,7,10,11,14,15},{16,17,20,21,24,25,28,29},{18..., dimensions={0} | all-to-all | bytes 294912 | tf_op jit(solution)/shard_map/all_to_all | solution.py:332
  40.9 0.0 collective-permute-done.5.partner_ref
  40.9 0.0 copy-done
  40.9 1.2 %shard_map.71 = bf16[8,4,5376]{2,1,0:T(4,128)(2,1)S(1)} custom-call(bf16[8,1,72,128]{3,2,1,0:T(8,128)(2,1)S(1)} %all_to_all.16.part_ref, bf16[256,5376]{1,0:T(8,128)(2,1)S(1)} %copy-done, bf16[256,5376]{1,0:T(8,128)(2,1)S(1)} %collective-permute-done.5.partner_ref), custom_call_target="tpu_custom_call" | custom-call | tf_op jit(solution)/shard_map/pallas_call | solution.py:299
  42.1 15.0 %all_to_all.17.terms_ref = bf16[8,4,5376]{2,1,0:T(4,128)(2,1)S(1)} all-to-all(bf16[8,4,5376]{2,1,0:T(4,128)(2,1)S(1)} %shard_map.71), channel_id=1, replica_groups={{0,2,4,6,8,10,12,14},{1,3,5,7,9,11,13,15},{16,18,20,22,24,26,28,30},{17..., dimensions={0} | all-to-all | bytes 688128 | tf_op jit(solution)/shard_map/all_to_all | solution.py:332
  57.1 0.0 copy-done.2
  57.1 0.8 %shard_map.72 = f32[4,5376]{1,0:T(4,128)} custom-call(bf16[8,4,5376]{2,1,0:T(4,128)(2,1)S(1)} %all_to_all.17.terms_ref, bf16[4,5376]{1,0:T(4,128)(2,1)S(1)} %copy-done.1, f32[5376]{0:T(1024)S(1)} %copy-done.2), custom_call_target="tpu_custom_call" | custom-call | tf_op jit(solution)/shard_map/pallas_call | solution.py:356
  (9 shorter events, 0.0 us)
Async XLA Ops:
  0.0 1.6 %collective-permute-start = (bf16[4,4096]{1,0:T(4,128)(2,1)}, bf16[4,4096]{1,0:T(4,128)(2,1)S(1)}, u32[]{:S(2)}, u32[]{:S(2)}) collective-permute-start(bf16[4,4096]{1,0:T(4,128)(2,1)} %in_ref.1), channel_id=1, source_target_pairs={{0,1},{1,0},{2,3},{3,2},{4,5},{5,4},{6,7},{7,6},{8,9},{9,8},{10,11... | collective-permute-start | bytes 98312 | tf_op jit(solution)/shard_map/ppermute | solution.py:335
  0.5 40.4 %collective-permute-start.5 = (bf16[256,5376]{1,0:T(8,128)(2,1)}, bf16[256,5376]{1,0:T(8,128)(2,1)S(1)}, u32[]{:S(2)}, u32[]{:S(2)}) collective-permute-start(bf16[256,5376]{1,0:T(8,128)(2,1)} %weight_ref.1), channel_id=1, source_target_pairs={{0,1},{1,0},{2,3},{3,2},{4,5},{5,4},{6,7},{7,6},{8,9},{9,8},{10,11... | collective-permute-start | bytes 8257544 | tf_op jit(solution)/shard_map/ppermute | solution.py:335
  0.5 17.6 %slice-start = ((s8[8388608]{0:T(1024)(128)(4,1)}), s8[4194304]{0:T(1024)(128)(4,1)S(1)}, s32[]{:S(2)}) async-start(s8[8388608]{0:T(1024)(128)(4,1)} %bitcast.2), calls=%async_computation.3 | async-start | bytes 8388608
  0.5 17.6 %slice-start.2 = ((s8[8388608]{0:T(1024)(128)(4,1)}), s8[4194304]{0:T(1024)(128)(4,1)S(1)}, s32[]{:S(2)}) async-start(s8[8388608]{0:T(1024)(128)(4,1)} %bitcast.4), calls=%async_computation.5 | async-start | bytes 8388608
  1.4 16.6 %slice-start.1 = ((s8[8388608]{0:T(1024)(128)(4,1)}), s8[4194304]{0:T(1024)(128)(4,1)S(1)}, s32[]{:S(2)}) async-start(s8[8388608]{0:T(1024)(128)(4,1)} %bitcast.2), calls=%async_computation.4 | async-start | bytes 8388608
  1.5 16.6 %slice-start.3 = ((s8[8388608]{0:T(1024)(128)(4,1)}), s8[4194304]{0:T(1024)(128)(4,1)S(1)}, s32[]{:S(2)}) async-start(s8[8388608]{0:T(1024)(128)(4,1)} %bitcast.4), calls=%async_computation.6 | async-start | bytes 8388608
  18.1 2.3 %collective-permute-start.1 = (bf16[64,2048]{1,0:T(8,128)(2,1)S(1)}, bf16[64,2048]{1,0:T(8,128)(2,1)S(1)}, u32[]{:S(2)}, u32[]{:S(2)}) collective-permute-start(bf16[64,2048]{1,0:T(8,128)(2,1)S(1)} %bitcast.6), channel_id=1, source_target_pairs={{0,1},{1,0},{2,3},{3,2},{4,5},{5,4},{6,7},{7,6},{8,9},{9,8},{10,11... | collective-permute-start | bytes 786440 | tf_op jit(solution)/shard_map/ppermute | solution.py:335
  19.8 2.2 %collective-permute-start.2 = (bf16[4,136,128]{2,1,0:T(8,128)(2,1)S(1)}, bf16[4,136,128]{2,1,0:T(8,128)(2,1)S(1)}, u32[]{:S(2)}, u32[]{:S(2)}) collective-permute-start(bf16[4,136,128]{2,1,0:T(8,128)(2,1)S(1)} %shard_map.67), channel_id=1, source_target_pairs={{0,1},{1,0},{2,3},{3,2},{4,5},{5,4},{6,7},{7,6},{8,9},{9,8},{10,11... | collective-permute-start | bytes 417800 | tf_op jit(solution)/shard_map/ppermute | solution.py:335
  22.2 18.8 %copy-start = (bf16[256,5376]{1,0:T(8,128)(2,1)S(1)}, bf16[256,5376]{1,0:T(8,128)(2,1)}, u32[]{:S(2)}) copy-start(bf16[256,5376]{1,0:T(8,128)(2,1)} %weight_ref.1) | copy-start | bytes 8257540
  22.2 34.9 %copy-start.1 = (bf16[4,5376]{1,0:T(4,128)(2,1)S(1)}, bf16[4,5376]{1,0:T(4,128)(2,1)}, u32[]{:S(2)}) copy-start(bf16[4,5376]{1,0:T(4,128)(2,1)} %residual_ref.1) | copy-start | bytes 129028
  22.2 34.9 %copy-start.2 = (f32[5376]{0:T(1024)S(1)}, f32[5376]{0:T(1024)}, u32[]{:S(2)}) copy-start(f32[5376]{0:T(1024)} %gain_ref.1) | copy-start | bytes 64516
  25.2 1.6 %collective-permute-start.3 = (bf16[4,136,128]{2,1,0:T(8,128)(2,1)S(1)}, bf16[4,136,128]{2,1,0:T(8,128)(2,1)S(1)}, u32[]{:S(2)}, u32[]{:S(2)}) collective-permute-start(bf16[4,136,128]{2,1,0:T(8,128)(2,1)S(1)} %slice.4), channel_id=1, source_target_pairs={{0,1},{1,0},{2,3},{3,2},{4,5},{5,4},{6,7},{7,6},{8,9},{9,8},{10,11... | collective-permute-start | bytes 417800 | tf_op jit(solution)/shard_map/ppermute | solution.py:335
  25.3 6.1 %collective-permute-start.4 = (bf16[4,136,128]{2,1,0:T(8,128)(2,1)S(1)}, bf16[4,136,128]{2,1,0:T(8,128)(2,1)S(1)}, u32[]{:S(2)}, u32[]{:S(2)}) collective-permute-start(bf16[4,136,128]{2,1,0:T(8,128)(2,1)S(1)} %shard_map.68.refs_2_), channel_id=1, source_target_pairs={{0,2},{1,3},{2,0},{3,1},{4,6},{5,7},{6,4},{7,5},{8,10},{9,11},{10,... | collective-permute-start | bytes 417800 | tf_op jit(solution)/shard_map/ppermute | solution.py:335

commit v3 on v2

--- a/solution.py
+++ b/solution.py
@@ -48,27 +48,21 @@
     return lax.bitwise_xor(lax.rem(lax.axis_index("ctx"), 4), offset)
 
 
-def fetch_kernel(in_ref, out_ref, sem):
-    copy = pltpu.make_async_copy(in_ref, out_ref, sem)
-    copy.start()
-    copy.wait()
-
-
-def fetch(x):
-    return pl.pallas_call(
-        fetch_kernel,
-        out_shape=jax.ShapeDtypeStruct(x.shape, x.dtype),
-        in_specs=[pl.BlockSpec(memory_space=pltpu.HBM)],
-        out_specs=VMEM_SPEC,
-        scratch_shapes=[pltpu.SemaphoreType.DMA],
+def mark_kernel(out_ref):
+    out_ref[...] = jnp.zeros_like(out_ref)
+
+
+def mark(cover):
+    return pl.pallas_call(
+        mark_kernel,
+        out_shape=jax.ShapeDtypeStruct((8, 128), jnp.float32),
+        out_specs=VMEM_SPEC,
         compiler_params=params(2 << 20),
-        cost_estimate=pl.CostEstimate(
-            flops=0, bytes_accessed=64 * x.size * x.dtype.itemsize, transcendentals=0
-        ),
-    )(pltpu.with_memory_space_constraint(x, pltpu.HBM))
-
-
-def spread_kernel(own_width, own_ref, partner_ref, out_ref):
+        cost_estimate=pl.CostEstimate(flops=cover, bytes_accessed=0, transcendentals=0),
+    )()
+
+
+def spread_kernel(own_width, own_ref, partner_ref, mark_ref, out_ref):
     chips = out_ref.shape[0]
     slot = slot_of(1)
     parity = lax.rem(slot, 2)
@@ -90,11 +84,11 @@
         out_shape=jax.ShapeDtypeStruct(
             (chips, 2 * queries.shape[0], chips * own_width), queries.dtype
         ),
-        in_specs=[VMEM_SPEC] * 2,
+        in_specs=[VMEM_SPEC] * 3,
         out_specs=VMEM_SPEC,
         compiler_params=params(2 << 20),
         cost_estimate=pl.CostEstimate(flops=cover, bytes_accessed=0, transcendentals=0),
-    )(queries, partner_queries)
+    )(queries, partner_queries, mark(cover))
 
 
 def attend_kernel(
@@ -341,7 +335,7 @@
     cover = 4000 * keys.size * keys.dtype.itemsize
     partner_queries = swap(queries, 1)
     partner_weight = swap(out_weight, 1)
-    ahead = spread(fetch(queries), partner_queries, chips, out_weight.shape[0], cover)
+    ahead = spread(queries, partner_queries, chips, out_weight.shape[0], cover)
     theirs = exchange(ahead, same_core)
     theirs = theirs.reshape(n * own_units, theirs.shape[2])
     mine = swap(theirs, 1)

time: 58.1 us -> 58.2 us (level)
  Pallas kernels: 9.62 us -> 8.71 us
  waiting for transfers between devices: 4.7 us -> 5.58 us
    pallas_call x1, Pallas kernels: 0.92 us -> 0.01 us  [mark(): pl.pallas_call(mark_kernel, out_shape=jax.ShapeDtypeStruct((8, 128), jnp....]
    ppermute x6, waiting for transfers between devices: 4.7 us -> 5.58 us  [swap(): return lax.ppermute(x, 'ctx', [(i, i ^ offset) for i in range(n)])]
  transfers between devices with their start and end apart: 6 -> 6, of which waited for: 2 -> 2; matrix products, arithmetic and copies ran while one was open for 0% -> 0% of each run, Pallas kernels for 13% -> 12%
where the time goes in v3:
time: 58.2 us; the launch traced here: 57.9 us
  blocking collectives  40.8 us (70%)
  Pallas kernels  8.71 us (15%)
  waiting for transfers between devices  5.58 us (10%)
  starting transfers between devices  2.66 us (5%)
    all_to_all x3, blocking collectives, exchange(): return lax.all_to_all(x, 'ctx', 0, 0, axis_index_groups=groups)  40.8 us
    pallas_call x3, Pallas kernels, attend(): pl.pallas_call(functools.partial(attend_kernel, offsets, few, own_heads,...  6.4 us
    ppermute x6, waiting for transfers between devices, swap(): return lax.ppermute(x, 'ctx', [(i, i ^ offset) for i in range(n)])  5.58 us
    ppermute x6, starting transfers between devices, swap(): return lax.ppermute(x, 'ctx', [(i, i ^ offset) for i in range(n)])  2.66 us
    pallas_call x1, Pallas kernels, project(): pl.pallas_call(functools.partial(project_kernel, heads, head_dim, tile),...  1.2 us
  transfers between devices with their start and end apart: 6, of which 2 were waited for; matrix products, arithmetic and copies ran while one was open for 0% of the time, Pallas kernels for 12%

profile of v3, /device:TPU:0, one launch (start us, length us, event | category | flops | bytes accessed | tf_op | source)
XLA Modules:
  0.0 57.9 jit_solution(12691189371513382693)
XLA Ops:
  0.0 0.5 collective-permute-start
  0.5 0.1 collective-permute-start.5
  0.6 0.0 slice-start.3
  0.6 1.0 %collective-permute-done.partner_ref = bf16[4,4096]{1,0:T(4,128)(2,1)S(1)} collective-permute-done((bf16[4,4096]{1,0:T(4,128)(2,1)}, bf16[4,4096]{1,0:T(4,128)(2,1)S(1)}, u32[]{:S(2)}, u32[]{:S(2)}) %collective-permute-start) | collective-permute-done | bytes 32800 | tf_op jit(solution)/shard_map/ppermute | solution.py:329
  1.6 0.0 copy-done.3
  1.6 16.5 %all_to_all.15 = bf16[8,8,2048]{2,1,0:T(8,128)(2,1)S(1)} all-to-all(bf16[8,8,2048]{2,1,0:T(8,128)(2,1)S(1)} %shard_map.65), channel_id=1, replica_groups={{0,2,4,6,8,10,12,14},{1,3,5,7,9,11,13,15},{16,18,20,22,24,26,28,30},{17..., dimensions={0} | all-to-all | bytes 524288 | tf_op jit(solution)/shard_map/all_to_all | solution.py:326
  18.1 0.0 collective-permute-start.1
  18.1 0.0 slice-done
  18.1 0.0 slice-done.2
  18.1 0.0 slice-done.1
  18.1 0.0 slice-done.3
  18.1 1.7 %shard_map.67 = bf16[4,136,128]{2,1,0:T(8,128)(2,1)S(1)} custom-call(bf16[16,2048,128]{2,1,0:T(8,128)(2,1)S(1)} %bitcast.3, bf16[16,2048,128]{2,1,0:T(8,128)(2,1)S(1)} %bitcast.5, bf16[64,2048]{1,0:T(8,128)(2,1)S(1)} %bitcast.7), custom_call_target="tpu_custom_call" | custom-call | flops 536870912 | bytes 4194304 | tf_op jit(solution)/shard_map/pallas_call | solution.py:185
  19.8 0.5 collective-permute-start.2
  20.4 0.0 collective-permute-done.1.refs_0_.refs_1_
  20.4 1.7 %shard_map.66.refs_0_ = bf16[4,136,128]{2,1,0:T(8,128)(2,1)S(1)} custom-call(bf16[16,2048,128]{2,1,0:T(8,128)(2,1)S(1)} %bitcast.3, bf16[16,2048,128]{2,1,0:T(8,128)(2,1)S(1)} %bitcast.5, bf16[64,2048]{1,0:T(8,128)(2,1)S(1)} %collective-permute-done.1.refs_0_.refs_1_), custom_call_target="tpu_custom_call" | custom-call | flops 536870912 | bytes 4194304 | tf_op jit(solution)/shard_map/pallas_call | solution.py:185
  22.1 0.0 collective-permute-done.2.refs_1_
  22.1 0.1 shard_map.68.refs_2_
  22.2 0.0 copy-start
  22.2 0.0 copy-start.1
  22.2 0.0 copy-start.2
  22.2 3.0 %shard_map.69.refs_0_ = bf16[8,136,128]{2,1,0:T(8,128)(2,1)S(1)} custom-call(bf16[16,2048,128]{2,1,0:T(8,128)(2,1)S(1)} %bitcast.3, bf16[16,2048,128]{2,1,0:T(8,128)(2,1)S(1)} %bitcast.5, bf16[64,2048]{1,0:T(8,128)(2,1)S(1)} %bitcast.8, bf16[64,2048]{1,0:T(8,128)(2,1)S(1)} %collective-permute-done.1.refs_0_.refs_1_, bf16[4,136,128]{2,1,0:T(8,128)(2,1)S(1)} %shard_map.68.refs_2_), custom_call_target="tpu_custom_call" | custom-call | flops 1073741824 | bytes 8388608 | tf_op jit(solution)/shard_map/pallas_call | solution.py:185
  25.2 0.1 collective-permute-start.3
  25.3 1.5 %collective-permute-start.4 = (bf16[4,136,128]{2,1,0:T(8,128)(2,1)S(1)}, bf16[4,136,128]{2,1,0:T(8,128)(2,1)S(1)}, u32[]{:S(2)}, u32[]{:S(2)}) collective-permute-start(bf16[4,136,128]{2,1,0:T(8,128)(2,1)S(1)} %shard_map.68.refs_2_), channel_id=1, source_target_pairs={{0,2},{1,3},{2,0},{3,1},{4,6},{5,7},{6,4},{7,5},{8,10},{9,11},{10,... | collective-permute-start | bytes 417800 | tf_op jit(solution)/shard_map/ppermute | solution.py:329
  26.8 0.0 collective-permute-done.3.refs_1_
  26.8 4.6 %collective-permute-done.4.refs_2_ = bf16[4,136,128]{2,1,0:T(8,128)(2,1)S(1)} collective-permute-done((bf16[4,136,128]{2,1,0:T(8,128)(2,1)S(1)}, bf16[4,136,128]{2,1,0:T(8,128)(2,1)S(1)}, u32[]{:S(2)}, u32[]{:S(2)}) %collective-permute-start.4) | collective-permute-done | bytes 139296 | tf_op jit(solution)/shard_map/ppermute | solution.py:329
  31.4 0.2 shard_map.70
  31.6 9.4 %all_to_all.16.part_ref = bf16[8,1,72,128]{3,2,1,0:T(8,128)(2,1)S(1)} all-to-all(bf16[8,1,72,128]{3,2,1,0:T(8,128)(2,1)S(1)} %bitcast.9), channel_id=1, replica_groups={{0,1,4,5,8,9,12,13},{2,3,6,7,10,11,14,15},{16,17,20,21,24,25,28,29},{18..., dimensions={0} | all-to-all | bytes 294912 | tf_op jit(solution)/shard_map/all_to_all | solution.py:326
  40.9 0.0 collective-permute-done.5.partner_ref
  40.9 1.2 %shard_map.71 = bf16[8,4,5376]{2,1,0:T(4,128)(2,1)S(1)} custom-call(bf16[8,1,72,128]{3,2,1,0:T(8,128)(2,1)S(1)} %all_to_all.16.part_ref, bf16[256,5376]{1,0:T(8,128)(2,1)S(1)} %copy-done, bf16[256,5376]{1,0:T(8,128)(2,1)S(1)} %collective-permute-done.5.partner_ref), custom_call_target="tpu_custom_call" | custom-call | tf_op jit(solution)/shard_map/pallas_call | solution.py:293
  42.2 15.0 %all_to_all.17.terms_ref = bf16[8,4,5376]{2,1,0:T(4,128)(2,1)S(1)} all-to-all(bf16[8,4,5376]{2,1,0:T(4,128)(2,1)S(1)} %shard_map.71), channel_id=1, replica_groups={{0,2,4,6,8,10,12,14},{1,3,5,7,9,11,13,15},{16,18,20,22,24,26,28,30},{17..., dimensions={0} | all-to-all | bytes 688128 | tf_op jit(solution)/shard_map/all_to_all | solution.py:326
  57.1 0.0 copy-done.2
  57.1 0.8 %shard_map.72 = f32[4,5376]{1,0:T(4,128)} custom-call(bf16[8,4,5376]{2,1,0:T(4,128)(2,1)S(1)} %all_to_all.17.terms_ref, bf16[4,5376]{1,0:T(4,128)(2,1)S(1)} %copy-done.1, f32[5376]{0:T(1024)S(1)} %copy-done.2), custom_call_target="tpu_custom_call" | custom-call | tf_op jit(solution)/shard_map/pallas_call | solution.py:350
  (11 shorter events, 0.1 us)
Async XLA Ops:
  0.0 1.6 %copy-start.3 = (bf16[4,4096]{1,0:T(4,128)(2,1)S(1)}, bf16[4,4096]{1,0:T(4,128)(2,1)}, u32[]{:S(2)}) copy-start(bf16[4,4096]{1,0:T(4,128)(2,1)} %own_ref.1) | copy-start | bytes 98308
  0.0 1.6 %collective-permute-start = (bf16[4,4096]{1,0:T(4,128)(2,1)}, bf16[4,4096]{1,0:T(4,128)(2,1)S(1)}, u32[]{:S(2)}, u32[]{:S(2)}) collective-permute-start(bf16[4,4096]{1,0:T(4,128)(2,1)} %own_ref.1), channel_id=1, source_target_pairs={{0,1},{1,0},{2,3},{3,2},{4,5},{5,4},{6,7},{7,6},{8,9},{9,8},{10,11... | collective-permute-start | bytes 98312 | tf_op jit(solution)/shard_map/ppermute | solution.py:329
  0.5 40.4 %collective-permute-start.5 = (bf16[256,5376]{1,0:T(8,128)(2,1)}, bf16[256,5376]{1,0:T(8,128)(2,1)S(1)}, u32[]{:S(2)}, u32[]{:S(2)}) collective-permute-start(bf16[256,5376]{1,0:T(8,128)(2,1)} %weight_ref.1), channel_id=1, source_target_pairs={{0,1},{1,0},{2,3},{3,2},{4,5},{5,4},{6,7},{7,6},{8,9},{9,8},{10,11... | collective-permute-start | bytes 8257544 | tf_op jit(solution)/shard_map/ppermute | solution.py:329
  0.6 17.5 %slice-start = ((s8[8388608]{0:T(1024)(128)(4,1)}), s8[4194304]{0:T(1024)(128)(4,1)S(1)}, s32[]{:S(2)}) async-start(s8[8388608]{0:T(1024)(128)(4,1)} %bitcast.2), calls=%async_computation.3 | async-start | bytes 8388608
  0.6 17.5 %slice-start.2 = ((s8[8388608]{0:T(1024)(128)(4,1)}), s8[4194304]{0:T(1024)(128)(4,1)S(1)}, s32[]{:S(2)}) async-start(s8[8388608]{0:T(1024)(128)(4,1)} %bitcast.4), calls=%async_computation.5 | async-start | bytes 8388608
  0.6 17.5 %slice-start.1 = ((s8[8388608]{0:T(1024)(128)(4,1)}), s8[4194304]{0:T(1024)(128)(4,1)S(1)}, s32[]{:S(2)}) async-start(s8[8388608]{0:T(1024)(128)(4,1)} %bitcast.2), calls=%async_computation.4 | async-start | bytes 8388608
  0.6 17.5 %slice-start.3 = ((s8[8388608]{0:T(1024)(128)(4,1)}), s8[4194304]{0:T(1024)(128)(4,1)S(1)}, s32[]{:S(2)}) async-start(s8[8388608]{0:T(1024)(128)(4,1)} %bitcast.4), calls=%async_computation.6 | async-start | bytes 8388608
  18.1 2.3 %collective-permute-start.1 = (bf16[64,2048]{1,0:T(8,128)(2,1)S(1)}, bf16[64,2048]{1,0:T(8,128)(2,1)S(1)}, u32[]{:S(2)}, u32[]{:S(2)}) collective-permute-start(bf16[64,2048]{1,0:T(8,128)(2,1)S(1)} %bitcast.6), channel_id=1, source_target_pairs={{0,1},{1,0},{2,3},{3,2},{4,5},{5,4},{6,7},{7,6},{8,9},{9,8},{10,11... | collective-permute-start | bytes 786440 | tf_op jit(solution)/shard_map/ppermute | solution.py:329
  19.8 2.2 %collective-permute-start.2 = (bf16[4,136,128]{2,1,0:T(8,128)(2,1)S(1)}, bf16[4,136,128]{2,1,0:T(8,128)(2,1)S(1)}, u32[]{:S(2)}, u32[]{:S(2)}) collective-permute-start(bf16[4,136,128]{2,1,0:T(8,128)(2,1)S(1)} %shard_map.67), channel_id=1, source_target_pairs={{0,1},{1,0},{2,3},{3,2},{4,5},{5,4},{6,7},{7,6},{8,9},{9,8},{10,11... | collective-permute-start | bytes 417800 | tf_op jit(solution)/shard_map/ppermute | solution.py:329
  22.2 18.8 %copy-start = (bf16[256,5376]{1,0:T(8,128)(2,1)S(1)}, bf16[256,5376]{1,0:T(8,128)(2,1)}, u32[]{:S(2)}) copy-start(bf16[256,5376]{1,0:T(8,128)(2,1)} %weight_ref.1) | copy-start | bytes 8257540
  22.2 34.9 %copy-start.1 = (bf16[4,5376]{1,0:T(4,128)(2,1)S(1)}, bf16[4,5376]{1,0:T(4,128)(2,1)}, u32[]{:S(2)}) copy-start(bf16[4,5376]{1,0:T(4,128)(2,1)} %residual_ref.1) | copy-start | bytes 129028
  22.2 34.9 %copy-start.2 = (f32[5376]{0:T(1024)S(1)}, f32[5376]{0:T(1024)}, u32[]{:S(2)}) copy-start(f32[5376]{0:T(1024)} %gain_ref.1) | copy-start | bytes 64516
  25.2 1.6 %collective-permute-start.3 = (bf16[4,136,128]{2,1,0:T(8,128)(2,1)S(1)}, bf16[4,136,128]{2,1,0:T(8,128)(2,1)S(1)}, u32[]{:S(2)}, u32[]{:S(2)}) collective-permute-start(bf16[4,136,128]{2,1,0:T(8,128)(2,1)S(1)} %slice.4), channel_id=1, source_target_pairs={{0,1},{1,0},{2,3},{3,2},{4,5},{5,4},{6,7},{7,6},{8,9},{9,8},{10,11... | collective-permute-start | bytes 417800 | tf_op jit(solution)/shard_map/ppermute | solution.py:329
  25.3 6.1 %collective-permute-start.4 = (bf16[4,136,128]{2,1,0:T(8,128)(2,1)S(1)}, bf16[4,136,128]{2,1,0:T(8,128)(2,1)S(1)}, u32[]{:S(2)}, u32[]{:S(2)}) collective-permute-start(bf16[4,136,128]{2,1,0:T(8,128)(2,1)S(1)} %shard_map.68.refs_2_), channel_id=1, source_target_pairs={{0,2},{1,3},{2,0},{3,1},{4,6},{5,7},{6,4},{7,5},{8,10},{9,11},{10,... | collective-permute-start | bytes 417800 | tf_op jit(solution)/shard_map/ppermute | solution.py:329
